TPU v7x, 32 devices: a whole 2x2x4 slice. The times are simulated.
32 devices in a mesh: shard: 4 (over y, core), replica: 8 (over z, x).
Axes of the slice: x: 2, y: 2, z: 4, core: 2. Of those that a mesh axis runs over, the one named last changes fastest.
Arguments:
- tokens: bfloat16 [8, 1024, 1024], P('replica', 'shard'), may hold values from -6 to 6
- cotangent: bfloat16 [8, 1024, 1024], P('replica', 'shard'), may hold values from -6 to 6
- lengths: int32 [8], P('replica'), may hold values from 256 to 1024, as said below
- block_order: int32 [8, 8], P('replica'), may hold values from 0 to 7, as said below
- norm1_gain: bfloat16 [1024], P('shard'), may hold values from 0.099609375 to 1.8984375
- query_weight: bfloat16 [1024, 2048], P('shard'), may hold values from -0.1875 to 0.1875
- key_weight: bfloat16 [1024, 1024], P('shard'), may hold values from -0.1875 to 0.1875
- value_weight: bfloat16 [1024, 1024], P('shard'), may hold values from -0.1875 to 0.1875
- output_weight: bfloat16 [2048, 1024], P('shard'), may hold values from -1.5 to 1.5
- query_gain: bfloat16 [128], P('shard'), may hold values from 0.099609375 to 1.8984375
- key_gain: bfloat16 [128], P('shard'), may hold values from 0.099609375 to 1.8984375
- norm2_gain: bfloat16 [1024], P('shard'), may hold values from 0.099609375 to 1.8984375
- gate_weight: bfloat16 [1024, 3072], P('shard'), may hold values from -0.1875 to 0.1875
- up_weight: bfloat16 [1024, 3072], P('shard'), may hold values from -0.1875 to 0.1875
- down_weight: bfloat16 [3072, 1024], P('shard'), may hold values from -0.109375 to 0.109375
Outputs:
- output: bfloat16 [8, 1024, 1024], P('replica', 'shard')
- input_grad: float32 [8, 1024, 1024], P('replica', 'shard')
- norm1_gain_grad: float32 [1024], P('shard')
- query_weight_grad: float32 [1024, 2048], P('shard')
- key_weight_grad: float32 [1024, 1024], P('shard')
- value_weight_grad: float32 [1024, 1024], P('shard')
- output_weight_grad: float32 [2048, 1024], P('shard')
- query_gain_grad: float32 [128], P('shard')
- key_gain_grad: float32 [128], P('shard')
- norm2_gain_grad: float32 [1024], P('shard')
- gate_weight_grad: float32 [1024, 3072], P('shard')
- up_weight_grad: float32 [1024, 3072], P('shard')
- down_weight_grad: float32 [3072, 1024], P('shard')
Inputs may be any that keep to these rules, and one draw needn't show every extreme that they name: `lengths`: in every group of 1 sequence one has 1024 valid tokens; valid tokens hold positions 0 to length - 1. `block_order`: each row is a permutation of 0 to 7 in which places 2j and 2j + 1 hold blocks that add up to 7.
All inputs are finite; a program needn't handle non-finite values.
Results may differ from a plain program's by a relative error of at most 0.013.
Values may be sent and summed in bfloat16 or wider, within the bound.
A program may use at most 256 MiB of HBM per device.

v0:
```python
import jax
import jax.numpy as jnp
from jax import lax
from jax.sharding import PartitionSpec as P

EPSILON = 1e-06
ROPE_BASE = 1000000.0
BF = jnp.bfloat16
F32 = jnp.float32


def rms_scale(values, gain_vec):
    return (
        values * lax.rsqrt(jnp.mean(values * values, axis=-1, keepdims=True) + EPSILON) * gain_vec
    )


def rotate_half(values, cosine, sine_table):
    middle = values.shape[-1] // 2
    turned = jnp.concatenate([-values[..., middle:], values[..., :middle]], axis=-1)
    return values * cosine + turned * sine_table


def rotary_tables(position, head_width):
    middle = head_width // 2
    exponent = jnp.arange(middle, dtype=F32) * 2.0 / head_width
    inverse = ROPE_BASE ** (-exponent)
    phases = position.astype(F32)[..., None] * inverse
    phases = jnp.concatenate([phases, phases], axis=-1)
    return (jnp.cos(phases), jnp.sin(phases))


def mm(a, b):
    return jnp.einsum("ri,io->ro", a, b, preferred_element_type=F32)


def mm_t(a, b):
    return jnp.einsum("ro,io->ri", a, b, preferred_element_type=F32)


def mm_w(a, b):
    return jnp.einsum("ri,ro->io", a, b, preferred_element_type=F32)


def gather_rows(v):
    return lax.all_gather(v, "shard", axis=0, tiled=True)


def scatter_rows(v):
    return lax.psum_scatter(v.astype(BF), "shard", scatter_dimension=0, tiled=True).astype(F32)


def to_columns(w):
    return lax.all_to_all(w, "shard", split_axis=1, concat_axis=0, tiled=True)


def to_rows(g):
    return lax.all_to_all(g, "shard", split_axis=0, concat_axis=1, tiled=True)


def shards(
    tokens,
    cotangent,
    lengths,
    block_order,
    norm1_gain,
    query_weight,
    key_weight,
    value_weight,
    output_weight,
    query_gain,
    key_gain,
    norm2_gain,
    gate_weight,
    up_weight,
    down_weight,
):
    shard_count = lax.axis_size("shard")
    row_count = tokens.shape[1]
    block_count = block_order.shape[1]
    slot_len = row_count * shard_count
    block_len = slot_len // block_count
    head_width = query_gain.shape[0] * shard_count
    score_scale = head_width ** (-0.5)
    gains = lax.all_gather(
        jnp.concatenate([norm1_gain, norm2_gain, query_gain, key_gain]), "shard", axis=0
    )
    wide = norm1_gain.shape[0]
    gain_one = gains[:, :wide].reshape(-1).astype(F32)
    gain_two = gains[:, wide : 2 * wide].reshape(-1).astype(F32)
    gain_query = gains[:, 2 * wide : 2 * wide + query_gain.shape[0]].reshape(-1).astype(F32)
    gain_key = gains[:, 2 * wide + query_gain.shape[0] :].reshape(-1).astype(F32)
    w_qkv = tuple((to_columns(w) for w in (query_weight, key_weight, value_weight)))
    w_gate, w_up = (to_columns(gate_weight), to_columns(up_weight))
    heads = w_qkv[0].shape[1] // head_width
    kvs = w_qkv[1].shape[1] // head_width
    per = heads // kvs
    offsets = jnp.arange(slot_len, dtype=jnp.int32)
    pos_all = (
        jnp.repeat(block_order[0], block_len, total_repeat_length=slot_len) * block_len
        + offsets % block_len
    )
    pos_local = lax.dynamic_slice_in_dim(pos_all, lax.axis_index("shard") * row_count, row_count)
    valid_rows = (pos_local < lengths[0]).astype(F32)[:, None]
    allowed = pos_all[None, None, None, :] <= pos_all[None, None, :, None]
    inputs = tokens[0].astype(F32)
    normed_f, norm_one_back = jax.vjp(rms_scale, inputs, gain_one)
    normed = gather_rows(normed_f.astype(BF))
    grad_result = cotangent[0].astype(F32) * valid_rows
    grad_branch = gather_rows(grad_result.astype(BF))
    query_raw = mm(normed, w_qkv[0]).reshape(slot_len, heads, head_width)
    key_raw = mm(normed, w_qkv[1]).reshape(slot_len, kvs, head_width)
    value = mm(normed, w_qkv[2]).astype(BF).reshape(slot_len, kvs, head_width)
    cosine, sine = rotary_tables(pos_all, head_width)
    cosine, sine = (cosine[:, None, :], sine[:, None, :])

    def turn(q, k, gq, gk):
        return (
            rotate_half(rms_scale(q, gq), cosine, sine),
            rotate_half(rms_scale(k, gk), cosine, sine),
        )

    turned, turn_back = jax.vjp(turn, query_raw, key_raw, gain_query, gain_key)
    query = turned[0].astype(BF).reshape(slot_len, kvs, per, head_width)
    key = turned[1].astype(BF)

    def scores_of():
        raw = jnp.einsum("rkgd,tkd->kgrt", query, key, preferred_element_type=F32) * score_scale
        return jnp.where(allowed, raw, -1e30)

    scores = scores_of()
    row_top = jnp.max(scores, axis=-1, keepdims=True)
    log_total = row_top + jnp.log(jnp.sum(jnp.exp(scores - row_top), axis=-1, keepdims=True))
    probs = jnp.exp(scores - log_total).astype(BF)
    mixed = jnp.einsum("kgrt,tkd->rkgd", probs, value, preferred_element_type=F32)
    mixed = mixed.reshape(slot_len, heads * head_width).astype(BF)
    hidden = inputs + scatter_rows(mm(mixed, output_weight))
    normed2_f, norm_two_back = jax.vjp(rms_scale, hidden, gain_two)
    normed2 = gather_rows(normed2_f.astype(BF))
    active_f, swish_back = jax.vjp(
        lambda a, b: jax.nn.silu(a) * b, mm(normed2, w_gate), mm(normed2, w_up)
    )
    active = active_f.astype(BF)
    output = (valid_rows * (hidden + scatter_rows(mm(active, down_weight)))).astype(BF)
    grad_gate_f, grad_up_f = swish_back(mm_t(grad_branch, down_weight))
    grad_gate, grad_up = (grad_gate_f.astype(BF), grad_up_f.astype(BF))
    grad_hidden_norm, grad_gain_two = norm_two_back(
        scatter_rows(mm_t(grad_gate, w_gate) + mm_t(grad_up, w_up))
    )
    grad_hidden = grad_result + grad_hidden_norm
    grad_mixed_in = gather_rows(grad_hidden.astype(BF))
    grad_mixed = mm_t(grad_mixed_in, output_weight).astype(BF)
    grad_mixed = grad_mixed.reshape(slot_len, kvs, per, head_width)
    probs_f = jnp.exp(scores_of() - log_total)
    grad_probs = jnp.einsum("rkgd,tkd->kgrt", grad_mixed, value, preferred_element_type=F32)
    grad_value = jnp.einsum(
        "kgrt,rkgd->tkd", probs_f.astype(BF), grad_mixed, preferred_element_type=F32
    )
    row_inner = jnp.sum(probs_f * grad_probs, axis=-1, keepdims=True)
    grad_scores = (probs_f * (grad_probs - row_inner)).astype(BF)
    grad_query = (
        jnp.einsum("kgrt,tkd->rkgd", grad_scores, key, preferred_element_type=F32) * score_scale
    )
    grad_key = (
        jnp.einsum("kgrt,rkgd->tkd", grad_scores, query, preferred_element_type=F32) * score_scale
    )
    grad_query_raw, grad_key_raw, grad_gain_query, grad_gain_key = turn_back(
        (grad_query.reshape(slot_len, heads, head_width), grad_key)
    )
    grad_query_b = grad_query_raw.reshape(slot_len, -1).astype(BF)
    grad_key_b = grad_key_raw.reshape(slot_len, -1).astype(BF)
    grad_value_b = grad_value.reshape(slot_len, -1).astype(BF)
    grad_normed = (
        mm_t(grad_query_b, w_qkv[0]) + mm_t(grad_key_b, w_qkv[1]) + mm_t(grad_value_b, w_qkv[2])
    )
    grad_inputs_norm, grad_gain_one = norm_one_back(scatter_rows(grad_normed))
    input_grad = grad_hidden + grad_inputs_norm

    def total(v):
        return lax.psum(v.astype(BF), "replica").astype(F32)

    grad_down = total(mm_w(active, grad_branch))
    grad_gate_w = to_rows(total(mm_w(normed2, grad_gate)).astype(BF)).astype(F32)
    grad_up_w = to_rows(total(mm_w(normed2, grad_up)).astype(BF)).astype(F32)
    grad_output_w = total(mm_w(mixed, grad_mixed_in))
    grad_query_w = to_rows(total(mm_w(normed, grad_query_b)).astype(BF)).astype(F32)
    grad_key_w = to_rows(total(mm_w(normed, grad_key_b)).astype(BF)).astype(F32)
    grad_value_w = to_rows(total(mm_w(normed, grad_value_b)).astype(BF)).astype(F32)
    small = jnp.concatenate([grad_gain_one, grad_gain_two, grad_gain_query, grad_gain_key])
    small = lax.psum(small, ("shard", "replica"))
    at = lax.axis_index("shard")
    hw = query_gain.shape[0]

    def own(start, size):
        return lax.dynamic_slice_in_dim(small, start + at * size, size)

    model = wide * shard_count
    return (
        output[None],
        input_grad[None],
        own(0, wide),
        grad_query_w,
        grad_key_w,
        grad_value_w,
        grad_output_w,
        own(2 * model, hw),
        own(2 * model + head_width, hw),
        own(model, wide),
        grad_gate_w,
        grad_up_w,
        grad_down,
    )


def solution(mesh):
    rows, mat, vec = (P("replica", "shard", None), P("shard", None), P("shard"))
    placed = (rows, rows, P("replica"), P("replica", None), vec, mat, mat, mat, mat)
    placed += (vec, vec, vec, mat, mat, mat)
    outs = (rows, rows, vec, mat, mat, mat, mat, vec, vec, vec, mat, mat, mat)
    return jax.shard_map(shards, mesh=mesh, in_specs=placed, out_specs=outs, check_vma=False)
```

profile of v0, /device:TPU:0, one launch (start us, length us, event | category | flops | bytes accessed | tf_op | source)
XLA Modules:
  0.0 764.7 jit_solution(12287463658765484522)
XLA Ops:
  11.5 8.5 %all-reduce.4 = bf16[2304]{0:T(1024)(128)(2,1)S(1)} all-reduce(bf16[2304]{0:T(1024)(128)(2,1)S(1)} %dynamic-update-slice.3), channel_id=2, replica_groups=mesh['shard'=4,'replica'=8] {'shard'}, use_global_device_ids=true, to_apply=%add.4 | all-reduce | flops 2304 | bytes 9216
  23.4 3.5 all-to-all-start.1
  28.5 4.6 compare_select_fusion.1
  33.1 6.2 all-to-all-done.1
  39.3 4.1 all-to-all-start
  47.2 5.5 all-to-all-done
  52.7 4.3 all-to-all-start.2
  57.3 2.9 broadcast_multiply_fusion.2
  64.9 6.6 all-to-all-done.2
  82.9 3.4 fusion.4
  86.3 3.7 exponential_reduce_fusion
  92.0 6.1 convolution_convert_fusion.8
  98.1 3.9 convolution_convert_fusion
  102.1 31.8 %reduce-scatter.5.cloned.1.call-done = bf16[256,1024]{1,0:T(8,128)(2,1)} async-done(((bf16[1024,1024]{1,0:T(8,128)(2,1)}), bf16[256,1024]{1,0:T(8,128)(2,1)}) %reduce-scatter.5.cloned.1.call-update) | async-done | bytes 524304 | tf_op jit(solution)/shard_map/reduce_scatter | solution.py:50
  137.3 2.6 copy.111
  139.8 4.3 all-to-all-start.3
  147.0 2.6 copy.113
  149.6 25.8 %all-to-all-done.3 = bf16[256,4,768]{0,2,1:T(8,128)(2,1)} async-done(((bf16[256,4,768]{0,2,1:T(8,128)(2,1)}), bf16[256,4,768]{0,2,1:T(8,128)(2,1)}, u32[]{:S(2)}, u32[]{:S(2)}) %all-to-all-start.3) | async-done | bytes 1572896 | tf_op jit(solution)/shard_map/all_to_all | solution.py:54
  175.4 4.4 all-to-all-start.4
  179.9 2.8 copy.112
  182.7 28.1 %all-to-all-done.4 = bf16[256,4,768]{0,2,1:T(8,128)(2,1)} async-done(((bf16[256,4,768]{0,2,1:T(8,128)(2,1)}), bf16[256,4,768]{0,2,1:T(8,128)(2,1)}, u32[]{:S(2)}, u32[]{:S(2)}) %all-to-all-start.4) | async-done | bytes 1572896 | tf_op jit(solution)/shard_map/all_to_all | solution.py:54
  213.4 5.6 fusion.63
  219.0 3.5 fusion.62
  222.5 7.2 multiply_convert_fusion
  232.3 3.1 add_convert_fusion.1
  235.5 31.5 %reduce-scatter.9.cloned.1.call-done = bf16[256,1024]{1,0:T(8,128)(2,1)} async-done(((bf16[1024,1024]{1,0:T(8,128)(2,1)}), bf16[256,1024]{1,0:T(8,128)(2,1)}) %reduce-scatter.9.cloned.1.call-update) | async-done | bytes 524304 | tf_op jit(solution)/shard_map/reduce_scatter | solution.py:50
  268.7 2.6 fusion.53
  271.8 5.2 convolution_convert_fusion.3
  277.0 3.1 convolution_convert_fusion.4
  280.1 3.0 convolution_convert_fusion.2
  283.1 11.0 %all-gather.12.cloned.1.call-done = bf16[1024,1024]{1,0:T(8,128)(2,1)} async-done(((bf16[256,1024]{1,0:T(8,128)(2,1)}), bf16[1024,1024]{1,0:T(8,128)(2,1)}) %all-gather.12.cloned.1.call-update) | async-done | bytes 2097168 | tf_op jit(solution)/shard_map/all_gather | solution.py:46
  294.1 3.1 convolution_convert_fusion.7
  297.2 8.5 %fusion.18 = bf16[2,128,1024]{2,1,0:T(8,128)(2,1)S(1)} fusion(bf16[1024,2,2,128]{0,3,2,1:T(8,128)(2,1)S(1)} %bitcast.261, f32[2,1024,1024,2]{2,1,3,0:T(8,128)} %copy-done.1, f32[2,2,1024]{2,1,0:T(2,128)S(1)} %log_add_fusion, pred[1024,1024]{0,1:T(8,128)(4,1)S(1)} %broadcast_compare_fusion), kind=kOutput, calls=%fused_computation.65 | convolution fusion | flops 1090781184 | bytes 19415040 | tf_op jit(solution)/shard_map/kgrt,rkgd->tkd/dot_general | solution.py:156
  305.8 12.4 %fusion = (f32[2,2,1024]{2,1,0:T(2,128)S(1)}, f32[2,1024,1024,2]{2,1,3,0:T(8,128)}) fusion(f32[2,1024,1024,2]{2,1,3,0:T(8,128)} %copy-done.1, f32[2,2,1024]{2,1,0:T(2,128)S(1)} %log_add_fusion, pred[1024,1024]{0,1:T(8,128)(4,1)S(1)} %broadcast_compare_fusion, bf16[1024,2,128,1]{0,2,3,1:T(8,128)(2,1)S(1)} %bitcast.264, bf16[1024,2,2,128]{0,3,2,1:T(8,128)(2,1)S(1)} %bitcast.262), kind=kOutput, calls=%fused_computation.2 | convolution fusion | flops 1094709248 | bytes 36208640 | tf_op jit(solution)/shard_map/rkgd,tkd->kgrt/dot_general | solution.py:155
  318.2 12.4 %fusion.2 = bf16[2,2,1024,1024]{2,3,1,0:T(8,128)(2,1)S(1)} fusion(f32[2,1024,1024,2]{2,1,3,0:T(8,128)} %get-tuple-element.84, f32[2,1024,1024,2]{2,1,3,0:T(8,128)} %copy-done.1, f32[2,2,1024]{2,1,0:T(2,128)S(1)} %get-tuple-element.83, f32[2,2,1024]{2,1,0:T(2,128)S(1)} %log_add_fusion, pred[1024,1024]{0,1:T(8,128)(4,1)S(1)} %broadcast_compare_fusion), kind=kLoop, calls=%fused_computation.4 | loop fusion | flops 25165824 | bytes 43024384 | tf_op jit(solution)/shard_map/convert_element_type | solution.py:160
  332.0 2.9 broadcast_multiply_fusion
  354.6 3.9 add_convert_fusion
  358.5 4.5 convolution_convert_fusion.1
  363.1 247.1 %all-reduce.8.cloned.1.call-done = (bf16[4,256,512]{2,1,0:T(8,128)(2,1)}, bf16[4,256,256]{2,1,0:T(8,128)(2,1)}, bf16[4,256,256]{2,1,0:T(8,128)(2,1)}, bf16[512,1...) async-done(((bf16[4,256,512]{2,1,0:T(8,128)(2,1)}, bf16[4,256,256]{2,1,0:T(8,128)(2,1)}, ...) | async-done | bytes 7864336 | tf_op jit(solution)/shard_map/psum | solution.py:180
  610.2 13.2 %all_to_all.160 = bf16[4,256,256]{2,1,0:T(8,128)(2,1)} all-to-all(bf16[4,256,256]{2,1,0:T(8,128)(2,1)} %get-tuple-element.34), channel_id=1, replica_groups=mesh['shard'=4,'replica'=8] {'shard'}, dimensions={0} | all-to-all | bytes 1048576 | tf_op jit(solution)/shard_map/all_to_all | solution.py:58
  623.4 18.6 %all_to_all.161 = bf16[4,256,256]{2,1,0:T(8,128)(2,1)} all-to-all(bf16[4,256,256]{2,1,0:T(8,128)(2,1)} %get-tuple-element.35), channel_id=1, replica_groups=mesh['shard'=4,'replica'=8] {'shard'}, dimensions={0} | all-to-all | bytes 1048576 | tf_op jit(solution)/shard_map/all_to_all | solution.py:58
  642.0 17.6 %all_to_all.162 = bf16[4,256,512]{2,1,0:T(8,128)(2,1)} all-to-all(bf16[4,256,512]{2,1,0:T(8,128)(2,1)S(1)} %copy-done.34), channel_id=1, replica_groups=mesh['shard'=4,'replica'=8] {'shard'}, dimensions={0} | all-to-all | bytes 2097152 | tf_op jit(solution)/shard_map/all_to_all | solution.py:58
  659.6 4.5 all-to-all-start.9
  665.7 62.1 %psum.56 = f32[2304]{0:T(1024)S(1)} all-reduce(f32[2304]{0:T(1024)S(1)} %pad_maximum_fusion.1), channel_id=1, replica_groups=mesh['shard'=4,'replica'=8] {'shard','replica'}, use_global_device_ids=true, to_apply=%region_19.20 | all-reduce | flops 2304 | bytes 18432 | tf_op jit(solution)/shard_map/psum | solution.py:190
  728.5 3.4 fusion.30
  731.9 3.6 all-to-all-start.8
  736.0 2.8 convert_element_type.304
  749.1 6.4 all-to-all-done.8
  (215 shorter events, 80.0 us)
Async XLA Ops:
  7.2 215.3 %copy-start = (bf16[768,1024]{1,0:T(8,128)(2,1)S(1)}, bf16[768,1024]{1,0:T(8,128)(2,1)}, u32[]{:S(2)}) copy-start(bf16[768,1024]{1,0:T(8,128)(2,1)} %param.31) | copy-start | bytes 4718596
  7.2 15.0 %copy-start.39 = (bf16[256,1024]{1,0:T(8,128)(2,1)S(1)}, bf16[256,1024]{1,0:T(8,128)(2,1)}, u32[]{:S(2)}) copy-start(bf16[256,1024]{1,0:T(8,128)(2,1)} %param.23) | copy-start | bytes 1572868
  7.2 66.6 %all-gather.6.cloned.1.call-start = ((), (), s32[]{:S(2)}) async-start(), calls=%async_computation.14 | async-start | bytes 2621440 | tf_op jit(solution)/shard_map/all_gather | solution.py:46
  22.2 4.8 copy-start.40
  22.2 5.7 copy-start.41
  23.4 15.9 %all-to-all-start.1 = ((bf16[256,4,256]{2,0,1:T(8,128)(2,1)}), bf16[256,4,256]{2,0,1:T(8,128)(2,1)S(1)}, u32[]{:S(2)}, u32[]{:S(2)}) async-start(bf16[256,4,256]{2,0,1:T(8,128)(2,1)} %copy.103), calls=%async_computation.1 | async-start | bytes 1048576 | tf_op jit(solution)/shard_map/all_to_all | solution.py:54
  39.3 7.2 copy-start.13
  39.3 13.4 %all-to-all-start = ((bf16[256,4,256]{0,2,1:T(8,128)(2,1)}), bf16[256,4,256]{0,2,1:T(8,128)(2,1)}, u32[]{:S(2)}, u32[]{:S(2)}) async-start(bf16[256,4,256]{0,2,1:T(8,128)(2,1)} %bitcast.17), calls=%async_computation | async-start | bytes 1048576 | tf_op jit(solution)/shard_map/all_to_all | solution.py:54
  52.7 18.8 %all-to-all-start.2 = ((bf16[256,4,512]{2,0,1:T(8,128)(2,1)}), bf16[256,4,512]{2,0,1:T(8,128)(2,1)}, u32[]{:S(2)}, u32[]{:S(2)}) async-start(bf16[256,4,512]{2,0,1:T(8,128)(2,1)} %copy.106), calls=%async_computation.2 | async-start | bytes 2097152 | tf_op jit(solution)/shard_map/all_to_all | solution.py:54
  57.0 76.9 %reduce-scatter.5.cloned.1.call-start = ((), (), s32[]{:S(2)}) async-start(), calls=%async_computation.15 | async-start | bytes 2621440 | tf_op jit(solution)/shard_map/reduce_scatter | solution.py:50
  60.2 21.9 %copy-start.8 = (f32[1024,128]{0,1:T(8,128)}, f32[1024,128]{0,1:T(8,128)S(1)}, u32[]{:S(2)}) copy-start(f32[1024,128]{0,1:T(8,128)S(1)} %get-tuple-element.60) | copy-start | bytes 1572868
  76.2 4.3 copy-start.5
  76.2 2.3 copy-start.42
  82.8 3.4 copy-start.16
  86.3 5.8 copy-start.1
  86.3 3.7 copy-start.21
  90.8 7.3 copy-start.36
  92.0 6.1 copy-start.48
  102.0 31.9 %copy-start.4 = (bf16[1,256,1024]{2,1,0:T(8,128)(2,1)S(1)}, bf16[1,256,1024]{2,1,0:T(8,128)(2,1)}, u32[]{:S(2)}) copy-start(bf16[1,256,1024]{2,1,0:T(8,128)(2,1)} %param.17) | copy-start | bytes 1572868
  102.0 111.4 %all-gather.8.cloned.1.call-start = ((), (), s32[]{:S(2)}) async-start(), calls=%async_computation.16 | async-start | bytes 2621440 | tf_op jit(solution)/shard_map/all_gather | solution.py:46
  139.8 35.6 %all-to-all-start.3 = ((bf16[256,4,768]{0,2,1:T(8,128)(2,1)}), bf16[256,4,768]{0,2,1:T(8,128)(2,1)}, u32[]{:S(2)}, u32[]{:S(2)}) async-start(bf16[256,4,768]{0,2,1:T(8,128)(2,1)} %bitcast.234), calls=%async_computation.4 | async-start | bytes 3145728 | tf_op jit(solution)/shard_map/all_to_all | solution.py:54
  144.2 78.3 %all-gather.10.cloned.1.call-start = ((), (), s32[]{:S(2)}) async-start(), calls=%async_computation.18 | async-start | bytes 2621440 | tf_op jit(solution)/shard_map/all_gather | solution.py:46
  175.4 35.4 %all-to-all-start.4 = ((bf16[256,4,768]{0,2,1:T(8,128)(2,1)}), bf16[256,4,768]{0,2,1:T(8,128)(2,1)}, u32[]{:S(2)}, u32[]{:S(2)}) async-start(bf16[256,4,768]{0,2,1:T(8,128)(2,1)} %bitcast.235), calls=%async_computation.5 | async-start | bytes 3145728 | tf_op jit(solution)/shard_map/all_to_all | solution.py:54
  179.8 87.2 %reduce-scatter.9.cloned.1.call-start = ((), (), s32[]{:S(2)}) async-start(), calls=%async_computation.19 | async-start | bytes 2621440 | tf_op jit(solution)/shard_map/reduce_scatter | solution.py:50
  213.4 5.6 copy-start.30
  213.4 5.7 copy-start.44
  222.5 7.2 copy-start.31
  229.7 2.5 copy-start.32
  235.4 58.6 %all-gather.12.cloned.1.call-start = ((), (), s32[]{:S(2)}) async-start(), calls=%async_computation.20 | async-start | bytes 2621440 | tf_op jit(solution)/shard_map/all_gather | solution.py:46
  271.3 338.9 %all-reduce.8.cloned.1.call-start = ((), (), s32[]{:S(2)}) async-start(), calls=%async_computation.22 | async-start | bytes 15728640 | tf_op jit(solution)/shard_map/psum | solution.py:180
  271.8 5.2 copy-start.45
  271.8 5.2 copy-start.52
  277.0 3.1 copy-start.47
  277.0 3.1 copy-start.53
  297.2 8.5 %copy-start.37 = (bf16[1024,256]{0,1:T(8,128)(2,1)S(1)}, bf16[1024,256]{0,1:T(8,128)(2,1)}, u32[]{:S(2)}) copy-start(bf16[1024,256]{0,1:T(8,128)(2,1)} %copy-done.36) | copy-start | bytes 1572868
  305.8 39.2 %copy-start.38 = (bf16[2,128,1024]{2,1,0:T(8,128)(2,1)}, bf16[2,128,1024]{2,1,0:T(8,128)(2,1)S(1)}, u32[]{:S(2)}) copy-start(bf16[2,128,1024]{2,1,0:T(8,128)(2,1)S(1)} %fusion.18) | copy-start | bytes 1572868
  318.2 12.4 %copy-start.29 = (bf16[1024,2,128,1]{0,2,3,1:T(8,128)(2,1)S(1)}, bf16[1024,2,128,1]{0,2,3,1:T(8,128)(2,1)}, u32[]{:S(2)}) copy-start(bf16[1024,2,128,1]{0,2,3,1:T(8,128)(2,1)} %copy-done.28) | copy-start | bytes 1572868
  340.6 5.9 copy-start.25
  342.7 5.4 copy-start.19
  350.4 2.9 copy-start.14
  350.4 313.7 %reduce-scatter.11.cloned.1.call-start = ((), (), s32[]{:S(2)}) async-start(), calls=%async_computation.21 | async-start | bytes 2621440 | tf_op jit(solution)/shard_map/reduce_scatter | solution.py:50
  358.5 370.0 %reduce-scatter.7.cloned.1.call-start = ((), (), s32[]{:S(2)}) async-start(), calls=%async_computation.17 | async-start | bytes 2621440 | tf_op jit(solution)/shard_map/reduce_scatter | solution.py:50
  610.2 31.7 %copy-start.34 = (bf16[4,256,512]{2,1,0:T(8,128)(2,1)S(1)}, bf16[4,256,512]{2,1,0:T(8,128)(2,1)}, u32[]{:S(2)}) copy-start(bf16[4,256,512]{2,1,0:T(8,128)(2,1)} %get-tuple-element.33) | copy-start | bytes 3145732
  659.6 68.9 %copy-start.7 = (bf16[256,1024]{1,0:T(8,128)(2,1)S(1)}, bf16[256,1024]{1,0:T(8,128)(2,1)}, u32[]{:S(2)}) copy-start(bf16[256,1024]{1,0:T(8,128)(2,1)} %reduce-scatter.5.cloned.1.call-done) | copy-start | bytes 1572868
  659.6 68.9 %copy-start.12 = (bf16[1,256,1024]{2,1,0:T(8,128)(2,1)S(1)}, bf16[1,256,1024]{2,1,0:T(8,128)(2,1)}, u32[]{:S(2)}) copy-start(bf16[1,256,1024]{2,1,0:T(8,128)(2,1)} %param.18) | copy-start | bytes 1572868
  659.6 72.2 %all-to-all-start.9 = ((bf16[4,256,768]{2,1,0:T(8,128)(2,1)}), bf16[4,256,768]{2,1,0:T(8,128)(2,1)}, u32[]{:S(2)}, u32[]{:S(2)}) async-start(bf16[4,256,768]{2,1,0:T(8,128)(2,1)} %get-tuple-element.38), calls=%async_computation.13 | async-start | bytes 3145728 | tf_op jit(solution)/shard_map/all_to_all | solution.py:58
  731.9 23.7 %all-to-all-start.8 = ((bf16[4,256,768]{2,1,0:T(8,128)(2,1)}), bf16[4,256,768]{2,1,0:T(8,128)(2,1)S(1)}, u32[]{:S(2)}, u32[]{:S(2)}) async-start(bf16[4,256,768]{2,1,0:T(8,128)(2,1)} %get-tuple-element.37), calls=%async_computation.12 | async-start | bytes 3145728 | tf_op jit(solution)/shard_map/all_to_all | solution.py:58
  735.4 3.4 copy-start.33
  (22 other events, 34.1 us)
Sparse Core Ops, SparseCore 0:
  22.3 26.2 all-gather.5
  102.1 31.7 reduce-scatter.4
  137.4 33.7 all-gather.7
  172.7 33.7 all-gather.9
  235.6 31.4 reduce-scatter.8
  271.5 22.5 all-gather.11
  350.6 259.6 all-reduce.7
  613.3 35.3 reduce-scatter.10
  652.0 42.2 reduce-scatter.6
where the time goes:
time: 769 us; the launch traced here: 765 us
  waiting for transfers between devices  400 us (52%)
  blocking collectives  120 us (16%)
  matrix products  97.4 us (13%)
  other arithmetic  56.2 us (7%)
  local copies, waits for them, and re-layouts  44.7 us (6%)
  starting transfers between devices  29.9 us (4%)
  between operations  16.3 us (2%)
    psum x1, waiting for transfers between devices, total(): return lax.psum(v.astype(BF), 'replica').astype(F32)  247 us
    all_to_all x5, waiting for transfers between devices, to_columns(): return lax.all_to_all(w, 'shard', split_axis=1, concat_axis=0, tiled=True)  72.1 us
    reduce_scatter x4, waiting for transfers between devices, scatter_rows(): lax.psum_scatter(v.astype(BF), 'shard', scatter_dimension=0, tiled=True)  63.4 us
    psum x1, blocking collectives, shards(): small = lax.psum(small, ('shard', 'replica'))  62.1 us
    all_to_all x3, blocking collectives, to_rows(): return lax.all_to_all(g, 'shard', split_axis=0, concat_axis=1, tiled=True)  49.4 us
    dot_general x7, matrix products, mm(): return jnp.einsum('ri,io->ro', a, b, preferred_element_type=F32)  22 us
    dot_general x7, matrix products, mm_t(): return jnp.einsum('ro,io->ri', a, b, preferred_element_type=F32)  21.9 us
    all_to_all x5, starting transfers between devices, to_columns(): return lax.all_to_all(w, 'shard', split_axis=1, concat_axis=0, tiled=True)  20.6 us
  transfers between devices with their start and end apart: 16, of which 10 were waited for; matrix products, arithmetic and copies ran while one was open for 11% of the time, Pallas kernels for 0%

commit v1 on v0

--- a/solution.py
+++ b/solution.py
@@ -177,7 +177,7 @@
     input_grad = grad_hidden + grad_inputs_norm
 
     def total(v):
-        return lax.psum(v.astype(BF), "replica").astype(F32)
+        return jnp.sum(lax.all_gather(v.astype(BF), axis_name="replica"), axis=0).astype(F32)
 
     grad_down = total(mm_w(active, grad_branch))
     grad_gate_w = to_rows(total(mm_w(normed2, grad_gate)).astype(BF)).astype(F32)

time: 769 us -> 1400 us (1.82)
  waiting for transfers between devices: 400 us -> 999 us
  blocking collectives: 120 us -> 48 us
  other arithmetic: 56.2 us -> 107 us
  local copies, waits for them, and re-layouts: 44.7 us -> 66.5 us
  matrix products: 97.4 us -> 119 us
    all_gather x0 -> x7, waiting for transfers between devices: none -> 810 us  [total(): lax.all_gather(v.astype(BF), axis_name='replica')]
    psum x1 -> x0, waiting for transfers between devices: 247 us -> none  [total(): return lax.psum(v.astype(BF), 'replica').astype(F32)]
    all_to_all x3 -> x0, blocking collectives: 49.4 us -> none  [to_rows(): return lax.all_to_all(g, 'shard', split_axis=0, concat_axis=1, tiled=True)]
    reduce_sum x0 -> x7, other arithmetic: none -> 44.1 us  [total(): jnp.sum(lax.all_gather(v.astype(BF), axis_name='replica'), axis=0)]
    reduce_scatter x4, waiting for transfers between devices: 63.4 us -> 94.1 us  [scatter_rows(): lax.psum_scatter(v.astype(BF), 'shard', scatter_dimension=0, tiled=True)]
    psum x1, blocking collectives: 62.1 us -> 39.5 us  [shards(): small = lax.psum(small, ('shard', 'replica'))]
    unnamed x118 -> x135, local copies, waits for them, and re-layouts: 20.5 us -> 38 us
  transfers between devices with their start and end apart: 16 -> 25, of which waited for: 10 -> 16; matrix products, arithmetic and copies ran while one was open for 11% -> 13% of each run, Pallas kernels for 0% -> 0%
where the time goes in v1:
time: 1400 us
  waiting for transfers between devices  999 us (71%)
  matrix products  119 us (8%)
  other arithmetic  107 us (8%)
  local copies, waits for them, and re-layouts  66.5 us (5%)
  blocking collectives  48 us (3%)
  starting transfers between devices  42.1 us (3%)
  between operations  16.4 us (1%)
    all_gather x7, waiting for transfers between devices, total(): lax.all_gather(v.astype(BF), axis_name='replica')  810 us
    reduce_scatter x4, waiting for transfers between devices, scatter_rows(): lax.psum_scatter(v.astype(BF), 'shard', scatter_dimension=0, tiled=True)  94.1 us
    all_to_all x5, waiting for transfers between devices, to_columns(): return lax.all_to_all(w, 'shard', split_axis=1, concat_axis=0, tiled=True)  72.6 us
    reduce_sum x7, other arithmetic, total(): jnp.sum(lax.all_gather(v.astype(BF), axis_name='replica'), axis=0)  44.1 us
    psum x1, blocking collectives, shards(): small = lax.psum(small, ('shard', 'replica'))  39.5 us
    unnamed x135, local copies, waits for them, and re-layouts  38 us
  transfers between devices with their start and end apart: 25, of which 16 were waited for; matrix products, arithmetic and copies ran while one was open for 13% of the time, Pallas kernels for 0%

profile of v1, /device:TPU:0, one launch (start us, length us, event | category | flops | bytes accessed | tf_op | source)
XLA Modules:
  0.0 1398.4 jit_solution(9857178563039373314)
XLA Ops:
  10.3 8.5 all-reduce.4
  28.6 4.6 compare_select_fusion.1
  33.1 6.2 all-to-all-done.1
  39.3 4.1 all-to-all-start
  47.2 5.5 all-to-all-done
  52.7 4.3 all-to-all-start.2
  65.1 6.4 all-to-all-done.2
  86.3 3.7 exponential_reduce_fusion
  92.1 15.9 %convolution_convert_fusion.8 = bf16[2,128,2,1024]{3,1,2,0:T(8,128)(2,1)} fusion(bf16[1024,2,128,1]{0,2,3,1:T(8,128)(2,1)S(1)} %bitcast.273, f32[2,1024,1024,2]{2,1,3,0:T(8,128)S(1)} %get-tuple-element.114, f32[2,2,1024]{2,1,0:T(2,128)S(1)} %log_add_fusion, pred[1024,1024]{0,1:T(8,128)(4,1)S(1)} %broadcast_compare_fusion), kind=kOutput, calls=%fused_computation.58 | convolution fusion | flops 1091043328 | bytes 19415040 | tf_op jit(solution)/shard_map/kgrt,tkd->rkgd/dot_general | solution.py:135
  108.0 3.9 convolution_convert_fusion
  112.0 31.8 %reduce-scatter.5.cloned.1.call-done = bf16[256,1024]{1,0:T(8,128)(2,1)} async-done(((bf16[1024,1024]{1,0:T(8,128)(2,1)}), bf16[256,1024]{1,0:T(8,128)(2,1)}) %reduce-scatter.5.cloned.1.call-update) | async-done | bytes 524304 | tf_op jit(solution)/shard_map/reduce_scatter | solution.py:50
  149.7 4.3 all-to-all-start.3
  159.5 25.8 %all-to-all-done.3 = bf16[256,4,768]{0,2,1:T(8,128)(2,1)} async-done(((bf16[256,4,768]{0,2,1:T(8,128)(2,1)}), bf16[256,4,768]{0,2,1:T(8,128)(2,1)}, u32[]{:S(2)}, u32[]{:S(2)}) %all-to-all-start.3) | async-done | bytes 1572896 | tf_op jit(solution)/shard_map/all_to_all | solution.py:54
  185.3 4.3 all-to-all-start.4
  192.4 28.7 %all-to-all-done.4 = bf16[256,4,768]{0,2,1:T(8,128)(2,1)} async-done(((bf16[256,4,768]{0,2,1:T(8,128)(2,1)}), bf16[256,4,768]{0,2,1:T(8,128)(2,1)}, u32[]{:S(2)}, u32[]{:S(2)}) %all-to-all-start.4) | async-done | bytes 1572896 | tf_op jit(solution)/shard_map/all_to_all | solution.py:54
  223.6 5.6 fusion.62
  232.8 7.3 multiply_convert_fusion
  245.8 31.5 %reduce-scatter.9.cloned.1.call-done = bf16[256,1024]{1,0:T(8,128)(2,1)} async-done(((bf16[1024,1024]{1,0:T(8,128)(2,1)}), bf16[256,1024]{1,0:T(8,128)(2,1)}) %reduce-scatter.9.cloned.1.call-update) | async-done | bytes 524304 | tf_op jit(solution)/shard_map/reduce_scatter | solution.py:50
  281.7 22.7 %all-gather.26.cloned.1.call-done = bf16[1024,1024]{1,0:T(8,128)(2,1)} async-done(((bf16[256,1024]{1,0:T(8,128)(2,1)}), bf16[1024,1024]{1,0:T(8,128)(2,1)}) %all-gather.26.cloned.1.call-update) | async-done | bytes 2097168 | tf_op jit(solution)/shard_map/all_gather | solution.py:46
  307.6 12.7 fusion
  320.4 12.6 fusion.2
  341.9 10.9 fusion.18
  355.3 4.8 convolution_multiply_fusion
  367.0 5.1 convolution_convert_fusion.4
  375.5 4.0 add_convert_fusion
  379.6 4.5 convolution_convert_fusion.1
  384.2 5.2 convolution_convert_fusion.3
  389.4 3.9 convolution_convert_fusion.5
  393.4 5.1 convolution_convert_fusion.2
  398.5 16.5 %all-gather.30.cloned.1.call-done = bf16[8192,256]{1,0:T(8,128)(2,1)} async-done(((bf16[1024,256]{1,0:T(8,128)(2,1)}), bf16[8192,256]{1,0:T(8,128)(2,1)}) %all-gather.30.cloned.1.call-update) | async-done | bytes 4194320 | tf_op jit(solution)/shard_map/all_gather | solution.py:180
  415.0 3.7 reduce_sum.257
  422.2 66.6 %all-gather.32.cloned.1.call-done = bf16[8192,256]{1,0:T(8,128)(2,1)} async-done(((bf16[1024,256]{1,0:T(8,128)(2,1)}), bf16[8192,256]{1,0:T(8,128)(2,1)}) %all-gather.32.cloned.1.call-update) | async-done | bytes 4194320 | tf_op jit(solution)/shard_map/all_gather | solution.py:180
  488.8 3.7 reduce_sum.258
  496.0 118.7 %all-gather.28.cloned.1.call-done = bf16[8192,512]{1,0:T(8,128)(2,1)} async-done(((bf16[1024,512]{1,0:T(8,128)(2,1)}), bf16[8192,512]{1,0:T(8,128)(2,1)}) %all-gather.28.cloned.1.call-update) | async-done | bytes 8388624 | tf_op jit(solution)/shard_map/all_gather | solution.py:180
  614.7 5.9 reduce_sum.256
  621.4 3.8 all-to-all-start.5
  625.2 166.8 %all-gather.36.cloned.1.call-done = bf16[8192,768]{1,0:T(8,128)(2,1)} async-done(((bf16[1024,768]{1,0:T(8,128)(2,1)}), bf16[8192,768]{1,0:T(8,128)(2,1)}) %all-gather.36.cloned.1.call-update) | async-done | bytes 12582928 | tf_op jit(solution)/shard_map/all_gather | solution.py:180
  792.0 7.9 reduce_sum.260
  800.9 4.5 all-to-all-start.8
  805.4 30.7 %reduce-scatter.11.cloned.1.call-done = bf16[256,1024]{1,0:T(8,128)(2,1)} async-done(((bf16[1024,1024]{1,0:T(8,128)(2,1)}), bf16[256,1024]{1,0:T(8,128)(2,1)}) %reduce-scatter.11.cloned.1.call-update) | async-done | bytes 524304 | tf_op jit(solution)/shard_map/reduce_scatter | solution.py:50
  837.6 39.5 %psum.7 = f32[2304]{0:T(1024)S(1)} all-reduce(f32[2304]{0:T(1024)S(1)} %pad_maximum_fusion.1), channel_id=1, replica_groups=mesh['shard'=4,'replica'=8] {'shard','replica'}, use_global_device_ids=true, to_apply=%region_19.20 | all-reduce | flops 2304 | bytes 18432 | tf_op jit(solution)/shard_map/psum | solution.py:190
  881.2 167.6 %all-gather.38.cloned.1.call-done = bf16[8192,768]{1,0:T(8,128)(2,1)} async-done(((bf16[1024,768]{1,0:T(8,128)(2,1)}), bf16[8192,768]{1,0:T(8,128)(2,1)}) %all-gather.38.cloned.1.call-update) | async-done | bytes 12582928 | tf_op jit(solution)/shard_map/all_gather | solution.py:180
  1048.8 7.9 reduce_sum.261
  1056.7 4.8 all-to-all-start.9
  1070.0 103.9 %all-gather.34.cloned.1.call-done = bf16[4096,1024]{1,0:T(8,128)(2,1)} async-done(((bf16[512,1024]{1,0:T(8,128)(2,1)}), bf16[4096,1024]{1,0:T(8,128)(2,1)}) %all-gather.34.cloned.1.call-update) | async-done | bytes 8388624 | tf_op jit(solution)/shard_map/all_gather | solution.py:180
  1173.9 5.7 reduce_sum.259
  1181.1 169.5 %all-gather.40.cloned.1.call-done = bf16[6144,1024]{1,0:T(8,128)(2,1)} async-done(((bf16[768,1024]{1,0:T(8,128)(2,1)}), bf16[6144,1024]{1,0:T(8,128)(2,1)}) %all-gather.40.cloned.1.call-update) | async-done | bytes 12582928 | tf_op jit(solution)/shard_map/all_gather | solution.py:180
  1350.6 9.3 reduce_sum.262
  (260 shorter events, 151.1 us)
Async XLA Ops:
  7.2 225.6 %copy-start = (bf16[768,1024]{1,0:T(8,128)(2,1)S(1)}, bf16[768,1024]{1,0:T(8,128)(2,1)}, u32[]{:S(2)}) copy-start(bf16[768,1024]{1,0:T(8,128)(2,1)} %param.31) | copy-start | bytes 4718596
  7.2 15.0 %copy-start.41 = (bf16[256,1024]{1,0:T(8,128)(2,1)S(1)}, bf16[256,1024]{1,0:T(8,128)(2,1)}, u32[]{:S(2)}) copy-start(bf16[256,1024]{1,0:T(8,128)(2,1)} %param.23) | copy-start | bytes 1572868
  7.2 66.6 %all-gather.20.cloned.1.call-start = ((), (), s32[]{:S(2)}) async-start(), calls=%async_computation.14 | async-start | bytes 2621440 | tf_op jit(solution)/shard_map/all_gather | solution.py:46
  22.2 5.7 copy-start.46
  23.5 15.9 %all-to-all-start.1 = ((bf16[256,4,256]{2,0,1:T(8,128)(2,1)}), bf16[256,4,256]{2,0,1:T(8,128)(2,1)S(1)}, u32[]{:S(2)}, u32[]{:S(2)}) async-start(bf16[256,4,256]{2,0,1:T(8,128)(2,1)} %copy.103), calls=%async_computation.1 | async-start | bytes 1048576 | tf_op jit(solution)/shard_map/all_to_all | solution.py:54
  39.3 7.0 copy-start.14
  39.3 13.4 all-to-all-start
  52.7 18.8 %all-to-all-start.2 = ((bf16[256,4,512]{2,0,1:T(8,128)(2,1)}), bf16[256,4,512]{2,0,1:T(8,128)(2,1)}, u32[]{:S(2)}, u32[]{:S(2)}) async-start(bf16[256,4,512]{2,0,1:T(8,128)(2,1)} %copy.106), calls=%async_computation.2 | async-start | bytes 2097152 | tf_op jit(solution)/shard_map/all_to_all | solution.py:54
  57.0 86.8 %reduce-scatter.5.cloned.1.call-start = ((), (), s32[]{:S(2)}) async-start(), calls=%async_computation.15 | async-start | bytes 2621440 | tf_op jit(solution)/shard_map/reduce_scatter | solution.py:50
  60.3 22.1 %copy-start.9 = (f32[1024,128]{0,1:T(8,128)}, f32[1024,128]{0,1:T(8,128)S(1)}, u32[]{:S(2)}) copy-start(f32[1024,128]{0,1:T(8,128)S(1)} %get-tuple-element.92) | copy-start | bytes 1572868
  86.3 5.8 copy-start.1
  90.8 17.2 %copy-start.37 = (bf16[1024,256]{0,1:T(8,128)(2,1)}, bf16[1024,256]{0,1:T(8,128)(2,1)S(1)}, u32[]{:S(2)}) copy-start(bf16[1024,256]{0,1:T(8,128)(2,1)S(1)} %convolution_convert_fusion.11) | copy-start | bytes 1572868
  92.1 16.0 %copy-start.56 = (bf16[512,1024]{1,0:T(8,128)(2,1)S(1)}, bf16[512,1024]{1,0:T(8,128)(2,1)}, u32[]{:S(2)}) copy-start(bf16[512,1024]{1,0:T(8,128)(2,1)} %param.25) | copy-start | bytes 3145732
  111.9 31.9 %copy-start.5 = (bf16[1,256,1024]{2,1,0:T(8,128)(2,1)S(1)}, bf16[1,256,1024]{2,1,0:T(8,128)(2,1)}, u32[]{:S(2)}) copy-start(bf16[1,256,1024]{2,1,0:T(8,128)(2,1)} %param.17) | copy-start | bytes 1572868
  111.9 111.7 %all-gather.22.cloned.1.call-start = ((), (), s32[]{:S(2)}) async-start(), calls=%async_computation.16 | async-start | bytes 2621440 | tf_op jit(solution)/shard_map/all_gather | solution.py:46
  149.7 35.6 %all-to-all-start.3 = ((bf16[256,4,768]{0,2,1:T(8,128)(2,1)}), bf16[256,4,768]{0,2,1:T(8,128)(2,1)}, u32[]{:S(2)}, u32[]{:S(2)}) async-start(bf16[256,4,768]{0,2,1:T(8,128)(2,1)} %bitcast.244), calls=%async_computation.4 | async-start | bytes 3145728 | tf_op jit(solution)/shard_map/all_to_all | solution.py:54
  154.1 78.7 %all-gather.24.cloned.1.call-start = ((), (), s32[]{:S(2)}) async-start(), calls=%async_computation.18 | async-start | bytes 2621440 | tf_op jit(solution)/shard_map/all_gather | solution.py:46
  185.3 35.7 %all-to-all-start.4 = ((bf16[256,4,768]{0,2,1:T(8,128)(2,1)}), bf16[256,4,768]{0,2,1:T(8,128)(2,1)}, u32[]{:S(2)}, u32[]{:S(2)}) async-start(bf16[256,4,768]{0,2,1:T(8,128)(2,1)} %bitcast.245), calls=%async_computation.5 | async-start | bytes 3145728 | tf_op jit(solution)/shard_map/all_to_all | solution.py:54
  189.7 87.7 %reduce-scatter.9.cloned.1.call-start = ((), (), s32[]{:S(2)}) async-start(), calls=%async_computation.19 | async-start | bytes 2621440 | tf_op jit(solution)/shard_map/reduce_scatter | solution.py:50
  223.6 5.7 copy-start.34
  223.6 5.7 copy-start.55
  232.8 7.3 copy-start.33
  245.7 58.6 %all-gather.26.cloned.1.call-start = ((), (), s32[]{:S(2)}) async-start(), calls=%async_computation.20 | async-start | bytes 2621440 | tf_op jit(solution)/shard_map/all_gather | solution.py:46
  281.6 133.3 %all-gather.30.cloned.1.call-start = ((), (), s32[]{:S(2)}) async-start(), calls=%async_computation.23 | async-start | bytes 4718592 | tf_op jit(solution)/shard_map/all_gather | solution.py:180
  307.6 12.8 copy-start.36
  320.3 12.6 copy-start.16
  320.4 12.6 copy-start.18
  341.4 147.4 %all-gather.32.cloned.1.call-start = ((), (), s32[]{:S(2)}) async-start(), calls=%async_computation.24 | async-start | bytes 4718592 | tf_op jit(solution)/shard_map/all_gather | solution.py:180
  341.9 11.7 copy-start.53
  355.2 259.5 %all-gather.28.cloned.1.call-start = ((), (), s32[]{:S(2)}) async-start(), calls=%async_computation.22 | async-start | bytes 9437184 | tf_op jit(solution)/shard_map/all_gather | solution.py:180
  366.9 5.4 copy-start.15
  366.9 425.1 %all-gather.36.cloned.1.call-start = ((), (), s32[]{:S(2)}) async-start(), calls=%async_computation.26 | async-start | bytes 14155776 | tf_op jit(solution)/shard_map/all_gather | solution.py:180
  372.1 464.0 %reduce-scatter.11.cloned.1.call-start = ((), (), s32[]{:S(2)}) async-start(), calls=%async_computation.21 | async-start | bytes 2621440 | tf_op jit(solution)/shard_map/reduce_scatter | solution.py:50
  379.5 498.2 %reduce-scatter.7.cloned.1.call-start = ((), (), s32[]{:S(2)}) async-start(), calls=%async_computation.17 | async-start | bytes 2621440 | tf_op jit(solution)/shard_map/reduce_scatter | solution.py:50
  384.2 664.6 %all-gather.38.cloned.1.call-start = ((), (), s32[]{:S(2)}) async-start(), calls=%async_computation.27 | async-start | bytes 14155776 | tf_op jit(solution)/shard_map/all_gather | solution.py:180
  389.4 784.5 %all-gather.34.cloned.1.call-start = ((), (), s32[]{:S(2)}) async-start(), calls=%async_computation.25 | async-start | bytes 9437184 | tf_op jit(solution)/shard_map/all_gather | solution.py:180
  393.3 957.3 %all-gather.40.cloned.1.call-start = ((), (), s32[]{:S(2)}) async-start(), calls=%async_computation.28 | async-start | bytes 14155776 | tf_op jit(solution)/shard_map/all_gather | solution.py:180
  418.7 73.8 %all-to-all-start.6 = ((bf16[4,256,256]{2,1,0:T(8,128)(2,1)}), bf16[4,256,256]{2,1,0:T(8,128)(2,1)S(1)}, u32[]{:S(2)}, u32[]{:S(2)}) async-start(bf16[4,256,256]{2,1,0:T(8,128)(2,1)} %bitcast.73), calls=%async_computation.10 | async-start | bytes 1048576 | tf_op jit(solution)/shard_map/all_to_all | solution.py:58
  492.5 128.1 %copy-start.25 = (bf16[4,256,256]{2,1,0:T(8,128)(2,1)}, bf16[4,256,256]{2,1,0:T(8,128)(2,1)S(1)}, u32[]{:S(2)}) copy-start(bf16[4,256,256]{2,1,0:T(8,128)(2,1)S(1)} %all-to-all-done.6) | copy-start | bytes 1572868
  492.5 128.1 %all-to-all-start.7 = ((bf16[4,256,256]{2,1,0:T(8,128)(2,1)}), bf16[4,256,256]{2,1,0:T(8,128)(2,1)S(1)}, u32[]{:S(2)}, u32[]{:S(2)}) async-start(bf16[4,256,256]{2,1,0:T(8,128)(2,1)} %bitcast.262), calls=%async_computation.11 | async-start | bytes 1048576 | tf_op jit(solution)/shard_map/all_to_all | solution.py:58
  621.4 178.5 %all-to-all-start.5 = ((bf16[4,256,512]{2,1,0:T(8,128)(2,1)}), bf16[4,256,512]{2,1,0:T(8,128)(2,1)S(1)}, u32[]{:S(2)}, u32[]{:S(2)}) async-start(bf16[4,256,512]{2,1,0:T(8,128)(2,1)} %bitcast.252), calls=%async_computation.9 | async-start | bytes 2097152 | tf_op jit(solution)/shard_map/all_to_all | solution.py:58
  799.9 36.2 %copy-start.45 = (f32[1,2,4,128]{3,1,2,0:T(2,128)S(1)}, f32[1,2,4,128]{3,1,2,0:T(2,128)}, u32[]{:S(2)}) copy-start(f32[1,2,4,128]{3,1,2,0:T(2,128)} %copy-done.44) | copy-start | bytes 12292
  799.9 36.2 %copy-start.48 = (f32[256]{0:T(256)S(1)}, f32[256]{0:T(256)}, u32[]{:S(2)}) copy-start(f32[256]{0:T(256)} %copy-done.47) | copy-start | bytes 3076
  800.9 76.9 %copy-start.50 = (f32[256]{0:T(256)S(1)}, f32[256]{0:T(256)}, u32[]{:S(2)}) copy-start(f32[256]{0:T(256)} %copy-done.49) | copy-start | bytes 3076
  800.9 76.9 %copy-start.8 = (bf16[256,1024]{1,0:T(8,128)(2,1)S(1)}, bf16[256,1024]{1,0:T(8,128)(2,1)}, u32[]{:S(2)}) copy-start(bf16[256,1024]{1,0:T(8,128)(2,1)} %reduce-scatter.5.cloned.1.call-done) | copy-start | bytes 1572868
  800.9 76.9 %copy-start.13 = (bf16[1,256,1024]{2,1,0:T(8,128)(2,1)S(1)}, bf16[1,256,1024]{2,1,0:T(8,128)(2,1)}, u32[]{:S(2)}) copy-start(bf16[1,256,1024]{2,1,0:T(8,128)(2,1)} %param.18) | copy-start | bytes 1572868
  800.9 255.9 %all-to-all-start.8 = ((bf16[4,256,768]{2,1,0:T(8,128)(2,1)}), bf16[4,256,768]{2,1,0:T(8,128)(2,1)}, u32[]{:S(2)}, u32[]{:S(2)}) async-start(bf16[4,256,768]{2,1,0:T(8,128)(2,1)} %bitcast.246), calls=%async_computation.12 | async-start | bytes 3145728 | tf_op jit(solution)/shard_map/all_to_all | solution.py:58
  1056.7 324.5 %all-to-all-start.9 = ((bf16[4,256,768]{2,1,0:T(8,128)(2,1)}), bf16[4,256,768]{2,1,0:T(8,128)(2,1)}, u32[]{:S(2)}, u32[]{:S(2)}) async-start(bf16[4,256,768]{2,1,0:T(8,128)(2,1)} %bitcast.247), calls=%async_computation.13 | async-start | bytes 3145728 | tf_op jit(solution)/shard_map/all_to_all | solution.py:58
  (37 other events, 92.5 us)
Sparse Core Ops, SparseCore 0:
  22.3 26.2 all-gather.19
  112.0 31.7 reduce-scatter.4
  147.3 33.7 all-gather.21
  183.2 33.8 all-gather.23
  245.9 31.4 reduce-scatter.8
  281.8 22.5 all-gather.25
  341.6 73.3 all-gather.29
  417.1 71.6 all-gather.31
  491.5 123.1 all-gather.27
  617.3 174.6 all-gather.35
  795.1 40.9 reduce-scatter.10
  839.2 30.3 reduce-scatter.6
  872.3 176.4 all-gather.37
  1050.8 123.1 all-gather.33
  1176.0 174.6 all-gather.39
